TPU v7x, 512 devices: a whole 4x4x16 slice. The times are simulated.
512 devices in a mesh: band: 16 (over x, y), region: 32 (over z, core).
Axes of the slice: x: 4, y: 4, z: 16, core: 2. Of those that a mesh axis runs over, the one named last changes fastest.
Arguments:
- state: bfloat16 [16, 32768], P(None, 'region'), may hold values from -4 to 4
- absorb_weight: bfloat16 [16, 16384], P(None, 'band'), may hold values from -1.5 to 1.5
- emit_weight: bfloat16 [16, 16384], P(None, 'band'), may hold values from -1.5 to 1.5
- path_len: float32 [8, 8192], P(None, 'region'), may hold values from 0.02 to 0.2
- crossing_slot: int32 [8, 8192], P(None, 'region'), may hold values from 0 to 4095, as said below
- request_rows: int32 [32, 32, 128], P('region'), may hold values from 0 to 1023
- cot_intensity: float32 [16384, 8192], P('band', 'region'), may hold values from -6 to 6
Outputs:
- grad_state: float32 [16, 32768], P(None, 'region')
Inputs may be any that keep to these rules, and one draw needn't show every extreme that they name: `crossing_slot`: within each ray block (the 256 rays of one index of region) the 2048 crossings take distinct slots; slot p * 128 + s names the cell listed at request_rows[block, p, s]. In every draw one region has all 128 of its slots taken by every ray block; the other listed slots are partly unused.
All inputs are finite; a program needn't handle non-finite values.
Results may differ from a plain program's by a relative error of at most 0.0051.
Values may be sent and summed in bfloat16 or wider, within the bound.
No kernel may reach another device: no remote copies, remote signals or barrier semaphores. Data moves between devices by JAX's collectives and lax.ppermute only.
A program may use at most 64 MiB of HBM per device.

v0:
```python
import jax
import jax.numpy as jnp
from jax import lax
from jax.sharding import PartitionSpec as P


def adjoint_block(absorb_x, emit_x, length, cot_block, w_abs, w_emit):
    depth_step = absorb_x.astype(jnp.float32) * length[None]
    passed = jnp.cumsum(depth_step, axis=1) - depth_step
    transmit = jnp.exp(-passed)
    emitted = emit_x.astype(jnp.float32) * length[None] * transmit
    behind = lax.cumsum(emitted, axis=1, reverse=True) - emitted
    grad_emit = (cot_block[:, None, :] * emitted).astype(jnp.bfloat16)
    grad_absorb = (-cot_block[:, None, :] * depth_step * behind).astype(jnp.bfloat16)
    bin_count = grad_emit.shape[0]
    grad_emit = grad_emit.reshape(bin_count, -1)
    grad_absorb = grad_absorb.reshape(bin_count, -1)
    return jnp.dot(w_abs, grad_absorb, preferred_element_type=jnp.float32) + jnp.dot(
        w_emit, grad_emit, preferred_element_type=jnp.float32
    )


def on_device(
    state, absorb_weight, emit_weight, path_len, crossing_slot, request_rows, cot_intensity
):
    bin_count = absorb_weight.shape[1]
    state_count = state.shape[0]
    cross_len = path_len.shape[0]
    ray_count = path_len.shape[1]
    wanted = lax.all_to_all(
        request_rows, "region", split_axis=1, concat_axis=0, tiled=True
    ).reshape(-1)
    slot_ids = crossing_slot.reshape(-1)
    picked = jnp.take(state, wanted, axis=1)
    arrived = lax.all_to_all(picked, "region", split_axis=1, concat_axis=1, tiled=True)
    state_x = jnp.take(arrived, slot_ids, axis=1)
    absorb_x = jnp.exp(
        jnp.dot(absorb_weight.T, state_x, preferred_element_type=jnp.float32)
    ).astype(jnp.bfloat16)
    emit_x = jnp.exp(jnp.dot(emit_weight.T, state_x, preferred_element_type=jnp.float32)).astype(
        jnp.bfloat16
    )
    bin_block = 256
    summed = jnp.zeros((state_count, cross_len * ray_count), jnp.float32)
    for first_bin in range(0, bin_count, bin_block):
        last_bin = first_bin + bin_block
        summed = summed + adjoint_block(
            absorb_x[first_bin:last_bin].reshape(bin_block, cross_len, ray_count),
            emit_x[first_bin:last_bin].reshape(bin_block, cross_len, ray_count),
            path_len,
            cot_intensity[first_bin:last_bin],
            absorb_weight[:, first_bin:last_bin],
            emit_weight[:, first_bin:last_bin],
        )
    sending = jnp.zeros((state_count, wanted.shape[0]), jnp.float32).at[:, slot_ids].set(summed)
    returned = lax.all_to_all(sending, "region", split_axis=1, concat_axis=1, tiled=True)
    partial_value = (
        jnp.zeros((state_count, state.shape[1]), jnp.float32).at[:, wanted].add(returned)
    )
    partial_value = lax.psum(partial_value, "band")
    return partial_value


def solution(mesh):
    return jax.shard_map(
        on_device,
        mesh=mesh,
        in_specs=(
            P(None, "region"),
            P(None, "band"),
            P(None, "band"),
            P(None, "region"),
            P(None, "region"),
            P("region", None, None),
            P("band", "region"),
        ),
        out_specs=P(None, "region"),
        check_vma=False,
    )
```

profile of v0, /device:TPU:32, one launch (start us, length us, event | category | flops | bytes accessed | tf_op | source)
XLA Modules:
  0.0 268.6 jit_solution(6498890352738340585)
XLA Ops:
  6.5 15.5 %all-to-all-start = ((s32[1,32,128]{2,0,1:T(1,128)}), s32[1,32,128]{2,0,1:T(1,128)S(1)}, u32[]{:S(2)}, u32[]{:S(2)}) async-start(s32[1,32,128]{2,0,1:T(1,128)} %bitcast.180), calls=%async_computation | async-start | bytes 32768 | tf_op jit(solution)/shard_map/all_to_all | solution.py:30
  22.0 0.7 copy.52
  22.7 0.6 compare_select_fusion.1
  23.3 0.9 copy.36
  24.3 8.9 %all-to-all-done = s32[1,32,128]{2,0,1:T(1,128)S(1)} async-done(((s32[1,32,128]{2,0,1:T(1,128)}), s32[1,32,128]{2,0,1:T(1,128)S(1)}, u32[]{:S(2)}, u32[]{:S(2)}) %all-to-all-start) | async-done | bytes 16416 | tf_op jit(solution)/shard_map/all_to_all | solution.py:30
  33.2 0.6 copy-done.5
  33.8 12.1 %gather_fusion = bf16[4096,16]{1,0:T(8,128)(2,1)S(1)} fusion(bf16[16,1024]{0,1:T(8,128)(2,1)S(1)} %copy.36, s32[4096]{0:T(1024)S(1)} %broadcast_clamp_fusion), kind=kCustom, calls=%fused_computation | custom fusion | bytes 278528 | tf_op jit(solution)/shard_map/jit(_take)/gather | solution.py:34
  46.3 0.7 broadcast_select_fusion.3
  47.0 5.0 %all-to-all-start.1 = ((bf16[16,32,128]{2,0,1:T(8,128)(2,1)}), bf16[16,32,128]{2,0,1:T(8,128)(2,1)S(1)}, u32[]{:S(2)}, u32[]{:S(2)}) async-start(bf16[16,32,128]{2,0,1:T(8,128)(2,1)} %broadcast_select_fusion.3), calls=%async_computation.1 | async-start | bytes 262144 | tf_op jit(solution)/shard_map/all_to_all | solution.py:35
  53.2 0.8 copy.43
  54.1 0.6 compare_and_fusion.1
  54.7 0.6 broadcast_clamp_fusion.1
  55.2 12.8 %all-to-all-done.1 = bf16[16,32,128]{2,0,1:T(8,128)(2,1)S(1)} async-done(((bf16[16,32,128]{2,0,1:T(8,128)(2,1)}), bf16[16,32,128]{2,0,1:T(8,128)(2,1)S(1)}, u32[]{:S(2)}, u32[]{:S(2)}) %all-to-all-start.1) | async-done | bytes 131104 | tf_op jit(solution)/shard_map/all_to_all | solution.py:35
  68.1 0.5 copy.38
  68.6 7.3 %gather_fusion.1 = bf16[2048,16]{1,0:T(8,128)(2,1)S(1)} fusion(bf16[16,4096]{0,1:T(8,128)(2,1)S(1)} %bitcast.166, s32[2048]{0:T(1024)} %broadcast_clamp_fusion.1), kind=kCustom, calls=%fused_computation.1 | custom fusion | bytes 139264 | tf_op jit(solution)/shard_map/jit(_take)/gather | solution.py:36
  75.9 2.4 fusion
  78.4 1.6 fusion.1
  80.0 0.7 slice_convert_fusion
  80.7 0.7 slice_convert_fusion.1
  82.1 0.9 fusion.35
  83.0 0.9 fusion.29
  84.0 2.5 fusion.5
  88.0 0.9 fusion.41
  89.0 0.9 fusion.47
  89.8 2.6 fusion.17
  95.2 6.2 %scatter_custom_fusion = f32[16,4096]{0,1:T(8,128)S(1)} fusion(s32[2048]{0:T(1024)} %bitcast.177, f32[2048,16]{1,0:T(8,128)S(1)} %copy.46, f32[]{:T(128)} %constant.41.clone.1), kind=kCustom, calls=%fused_computation.107 | custom fusion | bytes 262656 | tf_op jit(solution)/shard_map/scatter | solution.py:55
  101.4 0.6 copy.47
  102.0 25.2 %all_to_all.30 = f32[16,32,128]{2,0,1:T(8,128)S(1)} all-to-all(f32[16,32,128]{2,0,1:T(8,128)S(1)} %copy.47), channel_id=1, replica_groups=mesh['band'=16,'region'=32] {'region'}, dimensions={1} | all-to-all | bytes 524288 | tf_op jit(solution)/shard_map/all_to_all | solution.py:56
  127.1 0.6 copy.49
  127.8 23.3 %scatter_custom_fusion.1 = f32[16,1024]{0,1:T(8,128)} fusion(s32[4096]{0:T(1024)} %bitcast.173, f32[4096,16]{1,0:T(8,128)S(1)} %copy.49, f32[]{:T(128)} %constant.41.clone.1), kind=kCustom, calls=%fused_computation.111 | custom fusion | flops 65536 | bytes 66048 | tf_op jit(solution)/shard_map/scatter-add | solution.py:58
  151.0 108.9 %all-reduce.2.cloned.1.call-done = f32[16,1024]{0,1:T(8,128)} async-done(((f32[16,1024]{0,1:T(8,128)}), f32[16,1024]{0,1:T(8,128)}) %all-reduce.2.cloned.1.call-update) | async-done | bytes 65552 | tf_op jit(solution)/shard_map/psum | solution.py:60
  259.9 1.8 copy.50
  (47 shorter events, 6.4 us)
Async XLA Ops:
  6.5 45.5 %copy-start.1 = (f32[1024,256]{1,0:T(8,128)S(1)}, f32[1024,256]{1,0:T(8,128)}, u32[]{:S(2)}) copy-start(f32[1024,256]{1,0:T(8,128)} %param.13) | copy-start | bytes 3145732
  6.5 26.7 %all-to-all-start = ((s32[1,32,128]{2,0,1:T(1,128)}), s32[1,32,128]{2,0,1:T(1,128)S(1)}, u32[]{:S(2)}, u32[]{:S(2)}) async-start(s32[1,32,128]{2,0,1:T(1,128)} %bitcast.180), calls=%async_computation | async-start | bytes 32768 | tf_op jit(solution)/shard_map/all_to_all | solution.py:30
  33.2 0.6 copy-start.5
  46.3 5.9 %copy-start.2 = (f32[8,256]{1,0:T(8,128)S(1)}, f32[8,256]{1,0:T(8,128)}, u32[]{:S(2)}) copy-start(f32[8,256]{1,0:T(8,128)} %param.10) | copy-start | bytes 24580
  46.3 5.9 %copy-start.6 = (s32[8,256]{1,0:T(8,128)S(1)}, s32[8,256]{1,0:T(8,128)}, u32[]{:S(2)}) copy-start(s32[8,256]{1,0:T(8,128)} %param.11) | copy-start | bytes 24580
  47.0 21.1 %all-to-all-start.1 = ((bf16[16,32,128]{2,0,1:T(8,128)(2,1)}), bf16[16,32,128]{2,0,1:T(8,128)(2,1)S(1)}, u32[]{:S(2)}, u32[]{:S(2)}) async-start(bf16[16,32,128]{2,0,1:T(8,128)(2,1)} %broadcast_select_fusion.3), calls=%async_computation.1 | async-start | bytes 262144 | tf_op jit(solution)/shard_map/all_to_all | solution.py:35
  52.0 207.9 %all-reduce.2.cloned.1.call-start = ((), (), s32[]{:S(2)}) async-start(), calls=%async_computation.3 | async-start | bytes 1048576 | tf_op jit(solution)/shard_map/psum | solution.py:60
  52.3 2.4 copy-start.7
  75.9 2.4 copy-start.4
  75.9 2.4 copy-start.8
  83.0 1.0 copy-start
  84.0 2.6 copy-start.3
Sparse Core Ops, SparseCore 0:
  151.2 108.6 all-reduce.1
where the time goes:
time: 269 us
  waiting for transfers between devices  131 us (49%)
  other arithmetic  37.5 us (14%)
  local copies, waits for them, and re-layouts  33.9 us (13%)
  blocking collectives  25.2 us (9%)
  starting transfers between devices  20.5 us (8%)
  between operations  13.8 us (5%)
  matrix products  7.06 us (3%)
    psum x1, waiting for transfers between devices, on_device(): partial_value = lax.psum(partial_value, 'band')  109 us
    all_to_all x1, blocking collectives, on_device(): lax.all_to_all(sending, 'region', split_axis=1, concat_axis=1, tiled=True)  25.2 us
    scatter-add x1, other arithmetic, on_device(): jnp.zeros((state_count, state.shape[1]), jnp.float32).at[:, wanted]  23.3 us
    all_to_all x1, starting transfers between devices, on_device(): lax.all_to_all(request_rows, 'region', split_axis=1, concat_axis=0, tiled...  15.5 us
    all_to_all x1, waiting for transfers between devices, on_device(): lax.all_to_all(picked, 'region', split_axis=1, concat_axis=1, tiled=True)  12.8 us
    gather x2, local copies, waits for them, and re-layouts, on_device(): picked = jnp.take(state, wanted, axis=1)  12.5 us
    all_to_all x1, waiting for transfers between devices, on_device(): lax.all_to_all(request_rows, 'region', split_axis=1, concat_axis=0, tiled...  8.92 us
    gather x1, local copies, waits for them, and re-layouts, on_device(): state_x = jnp.take(arrived, slot_ids, axis=1)  7.34 us
  transfers between devices with their start and end apart: 3, of which 3 were waited for; matrix products, arithmetic and copies ran while one was open for 2% of the time, Pallas kernels for 0%

commit v1 on v0

--- a/solution.py
+++ b/solution.py
@@ -32,7 +32,12 @@
     ).reshape(-1)
     slot_ids = crossing_slot.reshape(-1)
     picked = jnp.take(state, wanted, axis=1)
-    arrived = lax.all_to_all(picked, "region", split_axis=1, concat_axis=1, tiled=True)
+    arrived = jnp.concatenate(
+        lax.all_to_all(
+            jnp.stack(jnp.split(picked, lax.axis_size("region"), axis=1)), "region", 0, 0
+        ),
+        axis=1,
+    )
     state_x = jnp.take(arrived, slot_ids, axis=1)
     absorb_x = jnp.exp(
         jnp.dot(absorb_weight.T, state_x, preferred_element_type=jnp.float32)

time: 269 us -> 292 us (1.086)
  local copies, waits for them, and re-layouts: 33.9 us -> 55.3 us
    unnamed x22 -> x53, local copies, waits for them, and re-layouts: 2.32 us -> 20.7 us
    another operation x0 -> x35, local copies, waits for them, and re-layouts: none -> 3.35 us  [on_device(): jnp.stack(jnp.split(picked, lax.axis_size('region'), axis=1))]
    gather x2 -> x1, local copies, waits for them, and re-layouts: 12.5 us -> 12.1 us  [on_device(): picked = jnp.take(state, wanted, axis=1)]
where the time goes in v1:
time: 292 us; the launch traced here: 291 us
  waiting for transfers between devices  131 us (45%)
  local copies, waits for them, and re-layouts  55.3 us (19%)
  other arithmetic  39 us (13%)
  blocking collectives  25.2 us (9%)
  starting transfers between devices  20.4 us (7%)
  between operations  13.8 us (5%)
  matrix products  7.07 us (2%)
    psum x1, waiting for transfers between devices, on_device(): partial_value = lax.psum(partial_value, 'band')  109 us
    all_to_all x1, blocking collectives, on_device(): lax.all_to_all(sending, 'region', split_axis=1, concat_axis=1, tiled=True)  25.2 us
    scatter-add x1, other arithmetic, on_device(): jnp.zeros((state_count, state.shape[1]), jnp.float32).at[:, wanted]  23.3 us
    unnamed x53, local copies, waits for them, and re-layouts  20.7 us
    all_to_all x1, starting transfers between devices, on_device(): lax.all_to_all(request_rows, 'region', split_axis=1, concat_axis=0, tiled...  15.4 us
    all_to_all x1, waiting for transfers between devices, on_device(): lax.all_to_all(jnp.stack(jnp.split(picked, lax.axis_size('region'), axis=...  12.8 us
    gather x1, local copies, waits for them, and re-layouts, on_device(): picked = jnp.take(state, wanted, axis=1)  12.1 us
    all_to_all x1, waiting for transfers between devices, on_device(): lax.all_to_all(request_rows, 'region', split_axis=1, concat_axis=0, tiled...  8.92 us
  transfers between devices with their start and end apart: 3, of which 3 were waited for; matrix products, arithmetic and copies ran while one was open for 2% of the time, Pallas kernels for 0%

profile of v1, /device:TPU:32, one launch (start us, length us, event | category | flops | bytes accessed | tf_op | source)
XLA Modules:
  0.0 291.3 jit_solution(16854786309509785310)
XLA Ops:
  6.5 15.4 %all-to-all-start = ((s32[1,32,128]{2,0,1:T(1,128)}), s32[1,32,128]{2,0,1:T(1,128)S(1)}, u32[]{:S(2)}, u32[]{:S(2)}) async-start(s32[1,32,128]{2,0,1:T(1,128)} %bitcast.244), calls=%async_computation | async-start | bytes 32768 | tf_op jit(solution)/shard_map/all_to_all | solution.py:30
  21.9 0.7 copy.114
  22.6 0.6 compare_select_fusion.1
  23.2 0.9 copy.67
  24.1 8.9 %all-to-all-done = s32[1,32,128]{2,0,1:T(1,128)S(1)} async-done(((s32[1,32,128]{2,0,1:T(1,128)}), s32[1,32,128]{2,0,1:T(1,128)S(1)}, u32[]{:S(2)}, u32[]{:S(2)}) %all-to-all-start) | async-done | bytes 16416 | tf_op jit(solution)/shard_map/all_to_all | solution.py:30
  33.1 0.6 copy-done.5
  33.7 12.1 %gather_fusion = bf16[4096,16]{1,0:T(8,128)(2,1)S(1)} fusion(bf16[16,1024]{0,1:T(8,128)(2,1)S(1)} %copy.67, s32[4096]{0:T(1024)S(1)} %broadcast_clamp_fusion), kind=kCustom, calls=%fused_computation | custom fusion | bytes 278528 | tf_op jit(solution)/shard_map/jit(_take)/gather | solution.py:34
  45.8 2.1 select_bitcast_fusion
  50.8 0.6 constant_dynamic-update-slice_fusion.31
  53.2 0.6 constant_dynamic-update-slice_fusion.27
  59.7 0.6 constant_dynamic-update-slice_fusion.16
  69.8 5.0 %all-to-all-start.1 = ((bf16[32,16,128]{2,1,0:T(8,128)(2,1)}), bf16[32,16,128]{2,1,0:T(8,128)(2,1)S(1)}, u32[]{:S(2)}, u32[]{:S(2)}) async-start(bf16[32,16,128]{2,1,0:T(8,128)(2,1)} %constant_dynamic-update-slice_fusion), calls=%async_computation.1 | async-start | bytes 262144 | tf_op jit(solution)/shard_map/all_to_all | solution.py:36
  76.0 0.8 copy.105
  76.8 0.6 compare_and_fusion.1
  78.0 12.8 %all-to-all-done.1 = bf16[32,16,128]{2,1,0:T(8,128)(2,1)S(1)} async-done(((bf16[32,16,128]{2,1,0:T(8,128)(2,1)}), bf16[32,16,128]{2,1,0:T(8,128)(2,1)S(1)}, u32[]{:S(2)}, u32[]{:S(2)}) %all-to-all-start.1) | async-done | bytes 131104 | tf_op jit(solution)/shard_map/all_to_all | solution.py:36
  91.3 7.3 %gather_fusion.1 = bf16[2048,16]{1,0:T(8,128)(2,1)S(1)} fusion(bf16[16,4096]{0,1:T(8,128)(2,1)S(1)} %bitcast.230, s32[2048]{0:T(1024)} %broadcast_clamp_fusion.1), kind=kCustom, calls=%fused_computation.1 | custom fusion | bytes 139264 | tf_op jit(solution)/shard_map/jit(_take)/gather | solution.py:41
  98.7 2.4 fusion
  101.1 1.6 fusion.1
  102.7 0.7 slice_convert_fusion
  103.4 0.7 slice_convert_fusion.1
  104.8 0.9 fusion.35
  105.8 0.9 fusion.29
  106.7 2.5 fusion.5
  110.8 0.9 fusion.41
  111.7 0.9 fusion.47
  112.6 2.6 fusion.17
  117.9 6.2 %scatter_custom_fusion = f32[16,4096]{0,1:T(8,128)S(1)} fusion(s32[2048]{0:T(1024)} %bitcast.241, f32[2048,16]{1,0:T(8,128)S(1)} %copy.108, f32[]{:T(128)} %constant.41.clone.1), kind=kCustom, calls=%fused_computation.108 | custom fusion | bytes 262656 | tf_op jit(solution)/shard_map/scatter | solution.py:60
  124.7 25.2 %all_to_all.26 = f32[16,32,128]{2,0,1:T(8,128)S(1)} all-to-all(f32[16,32,128]{2,0,1:T(8,128)S(1)} %copy.109), channel_id=1, replica_groups=mesh['band'=16,'region'=32] {'region'}, dimensions={1} | all-to-all | bytes 524288 | tf_op jit(solution)/shard_map/all_to_all | solution.py:61
  149.9 0.6 copy.111
  150.5 23.3 %scatter_custom_fusion.1 = f32[16,1024]{0,1:T(8,128)} fusion(s32[4096]{0:T(1024)} %bitcast.237, f32[4096,16]{1,0:T(8,128)S(1)} %copy.111, f32[]{:T(128)} %constant.41.clone.1), kind=kCustom, calls=%fused_computation.112 | custom fusion | flops 65536 | bytes 66048 | tf_op jit(solution)/shard_map/scatter-add | solution.py:63
  173.8 108.9 %all-reduce.2.cloned.1.call-done = f32[16,1024]{0,1:T(8,128)} async-done(((f32[16,1024]{0,1:T(8,128)}), f32[16,1024]{0,1:T(8,128)}) %all-reduce.2.cloned.1.call-update) | async-done | bytes 65552 | tf_op jit(solution)/shard_map/psum | solution.py:65
  282.7 1.8 copy.112
  (112 shorter events, 27.6 us)
Async XLA Ops:
  6.5 26.5 %all-to-all-start = ((s32[1,32,128]{2,0,1:T(1,128)}), s32[1,32,128]{2,0,1:T(1,128)S(1)}, u32[]{:S(2)}, u32[]{:S(2)}) async-start(s32[1,32,128]{2,0,1:T(1,128)} %bitcast.244), calls=%async_computation | async-start | bytes 32768 | tf_op jit(solution)/shard_map/all_to_all | solution.py:30
  33.1 0.6 copy-start.5
  48.0 26.8 %copy-start.1 = (f32[1024,256]{1,0:T(8,128)S(1)}, f32[1024,256]{1,0:T(8,128)}, u32[]{:S(2)}) copy-start(f32[1024,256]{1,0:T(8,128)} %param.13) | copy-start | bytes 3145732
  49.7 25.3 %copy-start.2 = (f32[8,256]{1,0:T(8,128)S(1)}, f32[8,256]{1,0:T(8,128)}, u32[]{:S(2)}) copy-start(f32[8,256]{1,0:T(8,128)} %param.10) | copy-start | bytes 24580
  49.7 25.3 %copy-start.6 = (s32[8,256]{1,0:T(8,128)S(1)}, s32[8,256]{1,0:T(8,128)}, u32[]{:S(2)}) copy-start(s32[8,256]{1,0:T(8,128)} %param.11) | copy-start | bytes 24580
  69.8 21.1 %all-to-all-start.1 = ((bf16[32,16,128]{2,1,0:T(8,128)(2,1)}), bf16[32,16,128]{2,1,0:T(8,128)(2,1)S(1)}, u32[]{:S(2)}, u32[]{:S(2)}) async-start(bf16[32,16,128]{2,1,0:T(8,128)(2,1)} %constant_dynamic-update-slice_fusion), calls=%async_computation.1 | async-start | bytes 262144 | tf_op jit(solution)/shard_map/all_to_all | solution.py:36
  74.7 207.9 %all-reduce.2.cloned.1.call-start = ((), (), s32[]{:S(2)}) async-start(), calls=%async_computation.3 | async-start | bytes 1048576 | tf_op jit(solution)/shard_map/psum | solution.py:65
  75.0 2.4 copy-start.7
  98.7 2.4 copy-start.4
  98.7 2.4 copy-start.8
  105.8 1.0 copy-start
  106.7 2.6 copy-start.3
Sparse Core Ops, SparseCore 0:
  173.9 108.6 all-reduce.1
